TPU v7x, 256 devices: a whole 4x4x8 slice. The times are simulated.
256 devices in a mesh: domain: 32 (over z, y_hi, core), band: 8 (over x, y_lo).
Axes of the slice: x: 4, y: 4 (y_hi: 2, y_lo: 2; y = y_hi * 2 + y_lo), z: 8, core: 2. Of those that a mesh axis runs over, the one named last changes fastest.
Arguments:
- orbitals: float32 [32, 192, 36864], P('band', 'domain'), may hold values from -6 to 6
- potential: float32 [192, 36864], P('domain'), may hold values from -1.5 to 1.5
- coefficients: float32 [32, 32], replicated, may hold values from -1.75 to 1.75
- owners: int32 [2], replicated, may hold values from 0 to 31
Outputs:
- filtered: float32 [32, 192, 36864], P('band', 'domain')
- rotated: float32 [32, 192, 36864], P('band', 'domain')
All inputs are finite; a program needn't handle non-finite values.
Results may differ from a plain program's by a relative error of at most 0.0001.
Values sent between devices are 32-bit elements; how exact they have to be, the bound alone decides.
No kernel may reach another device: no remote copies, remote signals or barrier semaphores. Data moves between devices by JAX's collectives and lax.ppermute only.
A program may use at most 256 MiB of HBM per device.

v0:
```python
import jax
import jax.numpy as jnp
from jax import lax
from jax.sharding import PartitionSpec as P

NZ = 192
DEG = 3
lap_coeffs = (-205.0 / 72.0, 8.0 / 5.0, -1.0 / 5.0, 8.0 / 315.0, -1.0 / 560.0)


def extended_2(x, sides, width):
    for axis, dim in sides:
        peers, length = (lax.axis_size(axis), x.shape[dim])
        up = [(i, (i + 1) % peers) for i in range(peers)]
        down = [(j, i) for i, j in up]
        last = lax.slice_in_dim(x, length - width, length, axis=dim)
        first = lax.slice_in_dim(x, 0, width, axis=dim)
        before = lax.ppermute(last, axis, up)
        after = lax.ppermute(first, axis, down)
        x = jnp.concatenate([before, x, after], axis=dim)
    return x


def spread(value, axis, source):
    kept = jnp.where(lax.axis_index(axis) == source, value, 0).astype(value.dtype)
    return lax.psum(kept, axis)


def hamiltonian(field, extended, potential):
    cells_x = field.shape[1]
    plane = field.shape[2]
    column_z = jnp.arange(plane) % NZ
    padded_y = jnp.pad(field, ((0, 0), (0, 0), (4 * NZ, 4 * NZ)))
    padded_z = jnp.pad(field, ((0, 0), (0, 0), (4, 4)))
    summed = 3.0 * lap_coeffs[0] * field
    for shift in range(1, 5):
        weight_k = lap_coeffs[shift]
        upper_ok = (column_z + shift < NZ).astype(field.dtype)
        lower_ok = (column_z - shift >= 0).astype(field.dtype)
        summed = summed + weight_k * (
            extended[:, 4 + shift : 4 + shift + cells_x]
            + extended[:, 4 - shift : 4 - shift + cells_x]
        )
        summed = summed + weight_k * (
            padded_y[:, :, (4 + shift) * NZ : (4 + shift) * NZ + plane]
            + padded_y[:, :, (4 - shift) * NZ : (4 - shift) * NZ + plane]
        )
        summed = summed + weight_k * (
            padded_z[:, :, 4 + shift : 4 + shift + plane] * upper_ok
            + padded_z[:, :, 4 - shift : 4 - shift + plane] * lower_ok
        )
    return -0.5 * summed + potential[None] * field


def chebyshev(block, potential, widen):
    previous = block
    current = (hamiltonian(block, widen(block), potential) - 6.0 * block) / 5.0
    for level in range(DEG - 1):
        following = (
            2.0 * (hamiltonian(current, widen(current), potential) - 6.0 * current) / 5.0 - previous
        )
        previous = current
        current = following
    return current


def widen_own(field):
    return extended_2(field, (("domain", 1),), 4)


def mixing(block, coefficients, source, target, width):
    part_coeffs = lax.dynamic_slice(coefficients, (source * width, target * width), (width, width))
    return jnp.einsum("bxp,bc->cxp", block, part_coeffs, precision=lax.Precision.HIGHEST)


def body(orbitals, potential, coefficients, owners):
    width = orbitals.shape[0]
    rounds_count = owners.shape[0]
    mine = lax.axis_index("band")
    sources = owners // width
    offsets = owners % width
    filtered = chebyshev(orbitals, potential, widen_own)
    rotated = mixing(filtered, coefficients, mine, mine, width)
    for turn in range(rounds_count):
        arrived = spread(filtered, "band", sources[turn])
        rolled = jnp.roll(arrived, -offsets[turn], axis=0)
        rotated = rotated + mixing(rolled, coefficients, sources[turn], mine, width)
    return (filtered, rotated)


def solution(mesh):
    in_specs = (P("band", "domain", None), P("domain", None), P(), P())
    out_specs = (P("band", "domain", None), P("band", "domain", None))
    return jax.shard_map(body, mesh=mesh, in_specs=in_specs, out_specs=out_specs, check_vma=False)
```

profile of v0, /device:TPU:4, one launch (start us, length us, event | category | flops | bytes accessed | tf_op | source)
XLA Modules:
  0.0 613.7 jit_solution(5512087887906080027)
XLA Ops:
  7.2 0.0 copy-start
  7.2 0.0 all-reduce.9.cloned.1.call-start
  7.2 2.7 fusion.148
  10.0 0.0 copy-start.1
  10.0 0.1 collective-permute-start.1
  10.1 8.0 %collective-permute-start = (f32[4,4,36864]{2,0,1:T(4,128)S(1)}, f32[4,4,36864]{2,0,1:T(4,128)S(1)}, u32[]{:S(2)}, u32[]{:S(2)}) collective-permute-start(f32[4,4,36864]{2,0,1:T(4,128)S(1)} %get-tuple-element.13), channel_id=1, source_target_pairs={{8,0},{16,8},{24,16},{32,24},{40,32},{48,40},{56,48},{64,56},{72,6... | collective-permute-start | bytes 7077896 | tf_op jit(solution)/shard_map/ppermute | solution.py:19
  18.1 0.1 fusion.125
  18.2 0.0 copy-start.7
  18.2 0.0 copy-start.8
  18.2 0.8 fusion.127
  19.0 0.8 fusion.129
  19.8 0.8 fusion.131
  20.5 24.1 %collective-permute-done.1 = f32[4,4,36864]{2,0,1:T(4,128)S(1)} collective-permute-done((f32[4,4,36864]{2,0,1:T(4,128)S(1)}, f32[4,4,36864]{2,0,1:T(4,128)S(1)}, u32[]{:S(2)}, u32[]{:S(2)}) %collective-permute-start.1) | collective-permute-done | bytes 2359328 | tf_op jit(solution)/shard_map/ppermute | solution.py:18
  44.6 0.2 constant_dynamic-update-slice_fusion.3
  44.8 0.0 copy-done.1
  44.8 1.1 constant_dynamic-update-slice_fusion.1
  45.9 0.0 collective-permute-done
  45.9 0.3 constant_dynamic-update-slice_fusion
  46.2 28.5 %broadcast_multiply_fusion = (f32[4,6,36864]{2,0,1:T(4,128)S(1)}, f32[4,6,36864]{2,0,1:T(4,128)}) fusion(f32[4,6,36864]{2,0,1:T(4,128)S(1)} %copy-done.1, f32[6,36864]{1,0:T(8,128)} %param.7, f32[36864]{0:T(1024)} %get-tuple-element.32, f32[36864]{0:T(1024)} %get-tuple-element.31, f32[4,10,36864]{2,0,1:T(4,128)S(1)} %get-tuple-element.16, ...), kind=kLoop, calls=%fused_computation.196 | loop fusion | flops 45121536 | bytes 40992768 | tf_op jit(solution)/shard_map/div | solution.py:57
  74.7 0.0 copy-start.5
  74.7 0.0 copy-start.4
  74.8 0.6 fusion.147
  75.4 4.2 collective-permute-start.2
  79.6 18.5 %collective-permute-start.3 = (f32[4,4,36864]{2,0,1:T(4,128)S(1)}, f32[4,4,36864]{2,0,1:T(4,128)S(1)}, u32[]{:S(2)}, u32[]{:S(2)}) collective-permute-start(f32[4,4,36864]{2,0,1:T(4,128)S(1)} %get-tuple-element.12), channel_id=1, source_target_pairs={{0,8},{8,16},{16,24},{24,32},{32,40},{40,48},{48,56},{56,64},{64,7... | collective-permute-start | bytes 7077896 | tf_op jit(solution)/shard_map/ppermute | solution.py:18
  98.0 0.1 broadcast_multiply_fusion.1
  98.2 7.8 %collective-permute-done.2 = f32[4,4,36864]{2,0,1:T(4,128)S(1)} collective-permute-done((f32[4,4,36864]{2,0,1:T(4,128)S(1)}, f32[4,4,36864]{2,0,1:T(4,128)S(1)}, u32[]{:S(2)}, u32[]{:S(2)}) %collective-permute-start.2) | collective-permute-done | bytes 2359328 | tf_op jit(solution)/shard_map/ppermute | solution.py:19
  106.0 25.2 %collective-permute-done.3 = f32[4,4,36864]{2,0,1:T(4,128)S(1)} collective-permute-done((f32[4,4,36864]{2,0,1:T(4,128)S(1)}, f32[4,4,36864]{2,0,1:T(4,128)S(1)}, u32[]{:S(2)}, u32[]{:S(2)}) %collective-permute-start.3) | collective-permute-done | bytes 2359328 | tf_op jit(solution)/shard_map/ppermute | solution.py:18
  131.2 0.0 copy-done.8
  131.3 26.8 %multiply_subtract_fusion.1 = f32[4,6,36864]{2,0,1:T(4,128)S(1)} fusion(f32[4,6,36864]{2,0,1:T(4,128)S(1)} %copy-done.1, f32[4,6,36864]{2,0,1:T(4,128)S(1)} %copy-done.4, f32[4,6,36864]{2,0,1:T(4,128)S(1)} %get-tuple-element.7, f32[4,4,36864]{2,0,1:T(4,128)S(1)} %collective-permute-done.3, f32[4,4,36864]{2,0,1:T(4,128)S(1)} %collective-permute-done.2, ...), kind=kLoop, calls=%fused_computation.142 | loop fusion | flops 53084160 | bytes 20938752 | tf_op jit(solution)/shard_map/sub | solution.py:60
  158.1 0.0 copy-start.2
  158.1 0.0 copy-start.16
  158.1 3.2 fusion.146
  161.3 0.1 copy-done.2
  161.4 0.0 collective-permute-start.4
  161.4 21.8 %collective-permute-start.5 = (f32[4,4,36864]{2,0,1:T(4,128)}, f32[4,4,36864]{2,0,1:T(4,128)}, u32[]{:S(2)}, u32[]{:S(2)}) collective-permute-start(f32[4,4,36864]{2,0,1:T(4,128)} %get-tuple-element.10), channel_id=1, source_target_pairs={{0,8},{8,16},{16,24},{24,32},{32,40},{40,48},{48,56},{56,64},{64,7... | collective-permute-start | bytes 7077896 | tf_op jit(solution)/shard_map/ppermute | solution.py:18
  183.2 0.0 copy-done.16
  183.2 0.7 fusion.149
  185.1 3.0 collective-permute-done.4
  188.0 1.4 copy-done.15
  189.5 23.9 %collective-permute-done.5 = f32[4,4,36864]{2,0,1:T(4,128)} collective-permute-done((f32[4,4,36864]{2,0,1:T(4,128)}, f32[4,4,36864]{2,0,1:T(4,128)}, u32[]{:S(2)}, u32[]{:S(2)}) %collective-permute-start.5) | collective-permute-done | bytes 2359328 | tf_op jit(solution)/shard_map/ppermute | solution.py:18
  213.3 46.0 %broadcast_select_fusion = (f32[4,6,36864]{2,0,1:T(4,128)}, f32[4,6,36864]{2,0,1:T(4,128)S(1)}) fusion(pred[]{:T(512)S(6)} %eq.15, f32[4,6,36864]{2,0,1:T(4,128)} %get-tuple-element.8, f32[4,6,36864]{2,0,1:T(4,128)} %copy-done.2, f32[6,36864]{1,0:T(8,128)} %param.7, f32[36864]{0:T(1024)} %get-tuple-element.32, f32[36864]{0:T(1024)} %get-tuple-element.31, ...), kind=kLoop, calls=%fused_computation.194 | loop fusion | flops 54853632 | bytes 20938752 | tf_op jit(solution)/shard_map/jit(_where)/select_n | solution.py:25
  259.3 0.0 copy-start.3
  259.3 3.0 broadcast_select_fusion.1
  262.4 0.0 all-reduce.9.cloned.1.call-update
  265.0 8.9 %fusion.136 = f32[4,6,36864]{2,0,1:T(4,128)} fusion(f32[4,6,36864]{2,0,1:T(4,128)S(1)} %get-tuple-element.6, f32[32,32]{1,0:T(8,128)S(1)} %copy-done, s32[]{:T(128)S(6)} %select_n.129), kind=kOutput, calls=%fused_computation.225 | convolution fusion | flops 42467328 | bytes 7079940 | tf_op jit(solution)/shard_map/bxp,bc->cxp/dot_general | solution.py:73
  274.0 308.8 %all-reduce.9.cloned.1.call-done = (f32[4,6,36864]{2,0,1:T(4,128)}, f32[4,6,36864]{2,0,1:T(4,128)}) async-done(((f32[4,6,36864]{2,0,1:T(4,128)}, f32[4,6,36864]{2,0,1:T(4,128)}), (f32[4,6,36864]{2,0,1:T(4,128)}, f32[4,6,36864]{2,0,1:T(4,128)})) %all-reduce.9.cloned.1.call-update) | async-done | bytes 7077904 | tf_op jit(solution)/shard_map/psum | solution.py:26
  582.8 12.4 %convolution_add_fusion.1 = f32[4,6,36864]{2,0,1:T(4,128)S(1)} fusion(f32[4,6,36864]{2,0,1:T(4,128)} %fusion.136, s32[]{:T(128)S(6)} %select_n.141, f32[4,6,36864]{2,0,1:T(4,128)} %get-tuple-element.3, f32[32,32]{1,0:T(8,128)S(1)} %copy-done, s32[]{:T(128)S(6)} %select_n.131, s32[]{:T(128)S(6)} %select_n.129), kind=kOutput, calls=%fused_computation.1 | convolution fusion | flops 44236800 | bytes 10618892 | tf_op jit(solution)/shard_map/bxp,bc->cxp/dot_general | solution.py:73
  595.2 11.7 %convolution_add_fusion = f32[4,6,36864]{2,0,1:T(4,128)} fusion(f32[4,6,36864]{2,0,1:T(4,128)S(1)} %convolution_add_fusion.1, s32[]{:T(128)S(6)} %select_n.143, f32[4,6,36864]{2,0,1:T(4,128)S(1)} %copy-done.6, f32[32,32]{1,0:T(8,128)S(1)} %copy-done, s32[]{:T(128)S(6)} %select_n.135, s32[]{:T(128)S(6)} %select_n.129), kind=kOutput, calls=%fused_computation | convolution fusion | flops 44236800 | bytes 10618892 | tf_op jit(solution)/shard_map/bxp,bc->cxp/dot_general | solution.py:73
  (21 shorter events, 0.1 us)
Async XLA Ops:
  7.2 257.9 %copy-start = (f32[32,32]{1,0:T(8,128)S(1)}, f32[32,32]{1,0:T(8,128)}, u32[]{:S(2)}) copy-start(f32[32,32]{1,0:T(8,128)} %param.8) | copy-start | bytes 12292
  7.2 575.6 %all-reduce.9.cloned.1.call-start = ((), (), s32[]{:S(2)}) async-start(), calls=%async_computation | async-start | bytes 14155776 | tf_op jit(solution)/shard_map/psum | solution.py:26
  10.0 34.8 %copy-start.1 = (f32[4,6,36864]{2,0,1:T(4,128)S(1)}, f32[4,6,36864]{2,0,1:T(4,128)}, u32[]{:S(2)}) copy-start(f32[4,6,36864]{2,0,1:T(4,128)} %param.6) | copy-start | bytes 10616836
  10.0 34.6 %collective-permute-start.1 = (f32[4,4,36864]{2,0,1:T(4,128)S(1)}, f32[4,4,36864]{2,0,1:T(4,128)S(1)}, u32[]{:S(2)}, u32[]{:S(2)}) collective-permute-start(f32[4,4,36864]{2,0,1:T(4,128)S(1)} %get-tuple-element.14), channel_id=1, source_target_pairs={{0,8},{8,16},{16,24},{24,32},{32,40},{40,48},{48,56},{56,64},{64,7... | collective-permute-start | bytes 7077896 | tf_op jit(solution)/shard_map/ppermute | solution.py:18
  10.1 35.9 %collective-permute-start = (f32[4,4,36864]{2,0,1:T(4,128)S(1)}, f32[4,4,36864]{2,0,1:T(4,128)S(1)}, u32[]{:S(2)}, u32[]{:S(2)}) collective-permute-start(f32[4,4,36864]{2,0,1:T(4,128)S(1)} %get-tuple-element.13), channel_id=1, source_target_pairs={{8,0},{16,8},{24,16},{32,24},{40,32},{48,40},{56,48},{64,56},{72,6... | collective-permute-start | bytes 7077896 | tf_op jit(solution)/shard_map/ppermute | solution.py:19
  18.2 113.0 %copy-start.7 = (f32[36864]{0:T(1024)}, f32[36864]{0:T(1024)S(1)}, u32[]{:S(2)}) copy-start(f32[36864]{0:T(1024)S(1)} %get-tuple-element.25) | copy-start | bytes 442372
  18.2 113.0 %copy-start.8 = (f32[36864]{0:T(1024)}, f32[36864]{0:T(1024)S(1)}, u32[]{:S(2)}) copy-start(f32[36864]{0:T(1024)S(1)} %get-tuple-element.26) | copy-start | bytes 442372
  19.0 112.3 %copy-start.9 = (f32[36864]{0:T(1024)}, f32[36864]{0:T(1024)S(1)}, u32[]{:S(2)}) copy-start(f32[36864]{0:T(1024)S(1)} %get-tuple-element.27) | copy-start | bytes 442372
  74.7 23.3 %copy-start.5 = (f32[6,36864]{1,0:T(8,128)S(1)}, f32[6,36864]{1,0:T(8,128)}, u32[]{:S(2)}) copy-start(f32[6,36864]{1,0:T(8,128)} %param.7) | copy-start | bytes 2654212
  74.7 56.5 %copy-start.4 = (f32[4,6,36864]{2,0,1:T(4,128)S(1)}, f32[4,6,36864]{2,0,1:T(4,128)}, u32[]{:S(2)}) copy-start(f32[4,6,36864]{2,0,1:T(4,128)} %get-tuple-element.8) | copy-start | bytes 10616836
  74.7 56.5 %copy-start.10 = (f32[36864]{0:T(1024)S(1)}, f32[36864]{0:T(1024)}, u32[]{:S(2)}) copy-start(f32[36864]{0:T(1024)} %get-tuple-element.28) | copy-start | bytes 442372
  74.8 56.5 %copy-start.11 = (f32[36864]{0:T(1024)S(1)}, f32[36864]{0:T(1024)}, u32[]{:S(2)}) copy-start(f32[36864]{0:T(1024)} %get-tuple-element.29) | copy-start | bytes 442372
  74.8 56.5 %copy-start.12 = (f32[36864]{0:T(1024)S(1)}, f32[36864]{0:T(1024)}, u32[]{:S(2)}) copy-start(f32[36864]{0:T(1024)} %get-tuple-element.30) | copy-start | bytes 442372
  74.8 56.5 %copy-start.13 = (f32[36864]{0:T(1024)S(1)}, f32[36864]{0:T(1024)}, u32[]{:S(2)}) copy-start(f32[36864]{0:T(1024)} %get-tuple-element.31) | copy-start | bytes 442372
  74.8 56.5 %copy-start.14 = (f32[36864]{0:T(1024)S(1)}, f32[36864]{0:T(1024)}, u32[]{:S(2)}) copy-start(f32[36864]{0:T(1024)} %get-tuple-element.32) | copy-start | bytes 442372
  75.4 30.6 %collective-permute-start.2 = (f32[4,4,36864]{2,0,1:T(4,128)S(1)}, f32[4,4,36864]{2,0,1:T(4,128)S(1)}, u32[]{:S(2)}, u32[]{:S(2)}) collective-permute-start(f32[4,4,36864]{2,0,1:T(4,128)S(1)} %get-tuple-element.11), channel_id=1, source_target_pairs={{8,0},{16,8},{24,16},{32,24},{40,32},{48,40},{56,48},{64,56},{72,6... | collective-permute-start | bytes 7077896 | tf_op jit(solution)/shard_map/ppermute | solution.py:19
  79.6 51.6 %collective-permute-start.3 = (f32[4,4,36864]{2,0,1:T(4,128)S(1)}, f32[4,4,36864]{2,0,1:T(4,128)S(1)}, u32[]{:S(2)}, u32[]{:S(2)}) collective-permute-start(f32[4,4,36864]{2,0,1:T(4,128)S(1)} %get-tuple-element.12), channel_id=1, source_target_pairs={{0,8},{8,16},{16,24},{24,32},{32,40},{40,48},{48,56},{56,64},{64,7... | collective-permute-start | bytes 7077896 | tf_op jit(solution)/shard_map/ppermute | solution.py:18
  158.1 3.3 copy-start.2
  158.1 25.1 %copy-start.16 = (s32[2]{0:T(128)S(1)}, s32[2]{0:T(128)}, u32[]{:S(2)}) copy-start(s32[2]{0:T(128)} %param.9) | copy-start | bytes 28
  161.4 26.7 %collective-permute-start.4 = (f32[4,4,36864]{2,0,1:T(4,128)}, f32[4,4,36864]{2,0,1:T(4,128)S(1)}, u32[]{:S(2)}, u32[]{:S(2)}) collective-permute-start(f32[4,4,36864]{2,0,1:T(4,128)} %get-tuple-element.9), channel_id=1, source_target_pairs={{8,0},{16,8},{24,16},{32,24},{40,32},{48,40},{56,48},{64,56},{72,6... | collective-permute-start | bytes 7077896 | tf_op jit(solution)/shard_map/ppermute | solution.py:19
  161.4 52.0 %collective-permute-start.5 = (f32[4,4,36864]{2,0,1:T(4,128)}, f32[4,4,36864]{2,0,1:T(4,128)}, u32[]{:S(2)}, u32[]{:S(2)}) collective-permute-start(f32[4,4,36864]{2,0,1:T(4,128)} %get-tuple-element.10), channel_id=1, source_target_pairs={{0,8},{8,16},{16,24},{24,32},{32,40},{40,48},{48,56},{56,64},{64,7... | collective-permute-start | bytes 7077896 | tf_op jit(solution)/shard_map/ppermute | solution.py:18
  188.0 1.4 copy-start.15
  259.3 5.7 copy-start.3
  582.7 12.4 %copy-start.6 = (f32[4,6,36864]{2,0,1:T(4,128)S(1)}, f32[4,6,36864]{2,0,1:T(4,128)}, u32[]{:S(2)}) copy-start(f32[4,6,36864]{2,0,1:T(4,128)} %get-tuple-element.4) | copy-start | bytes 10616836
Sparse Core Ops, SparseCore 0:
  262.5 320.1 all-reduce.8
where the time goes:
time: 614 us
  waiting for transfers between devices  393 us (64%)
  other arithmetic  107 us (17%)
  starting transfers between devices  52.6 us (9%)
  matrix products  33 us (5%)
  between operations  18.2 us (3%)
  local copies, waits for them, and re-layouts  10.3 us (2%)
    psum x1, waiting for transfers between devices, spread(): return lax.psum(kept, axis)  309 us
    ppermute x3, waiting for transfers between devices, extended_2(): before = lax.ppermute(last, axis, up)  73.2 us
    select_n x2, other arithmetic, spread(): jnp.where(lax.axis_index(axis) == source, value, 0).astype(value.dtype)  49 us
    ppermute x3, starting transfers between devices, extended_2(): before = lax.ppermute(last, axis, up)  40.4 us
    dot_general x3, matrix products, mixing(): jnp.einsum('bxp,bc->cxp', block, part_coeffs, precision=lax.Precision.HIG...  33 us
    div x1, other arithmetic, chebyshev(): current = (hamiltonian(block, widen(block), potential) - 6.0 * block) / 5.0  28.5 us
    sub x1, other arithmetic, chebyshev(): 2.0 * (hamiltonian(current, widen(current), potential) - 6.0 * current)  26.8 us
  transfers between devices with their start and end apart: 7, of which 6 were waited for; matrix products, arithmetic and copies ran while one was open for 2% of the time, Pallas kernels for 0%

commit v1 on v0

--- a/solution.py
+++ b/solution.py
@@ -23,7 +23,7 @@
 
 def spread(value, axis, source):
     kept = jnp.where(lax.axis_index(axis) == source, value, 0).astype(value.dtype)
-    return lax.psum(kept, axis)
+    return jnp.sum(lax.all_gather(kept, axis), axis=0)
 
 
 def hamiltonian(field, extended, potential):

time: 614 us -> 1860 us (3.03)
  waiting for transfers between devices: 393 us -> 1520 us
  other arithmetic: 107 us -> 211 us
  local copies, waits for them, and re-layouts: 10.3 us -> 36.9 us
    all_gather x0 -> x2, waiting for transfers between devices: none -> 1420 us  [spread(): return jnp.sum(lax.all_gather(kept, axis), axis=0)]
    psum x1 -> x0, waiting for transfers between devices: 309 us -> none  [spread(): return lax.psum(kept, axis)]
    sub x1, other arithmetic: 26.8 us -> 60.1 us  [chebyshev(): 2.0 * (hamiltonian(current, widen(current), potential) - 6.0 * current)]
    reduce_sum x0 -> x2, other arithmetic: none -> 32.5 us  [spread(): return jnp.sum(lax.all_gather(kept, axis), axis=0)]
    ppermute x3, waiting for transfers between devices: 10.8 us -> 37.9 us  [extended_2(): after = lax.ppermute(first, axis, down)]
    div x1, other arithmetic: 28.5 us -> 55.2 us  [chebyshev(): current = (hamiltonian(block, widen(block), potential) - 6.0 * block) / 5.0]
  transfers between devices with their start and end apart: 7 -> 8, of which waited for: 6 -> 8; matrix products, arithmetic and copies ran while one was open for 2% -> 2% of each run, Pallas kernels for 0% -> 0%
where the time goes in v1:
time: 1860 us
  waiting for transfers between devices  1520 us (82%)
  other arithmetic  211 us (11%)
  starting transfers between devices  43.5 us (2%)
  local copies, waits for them, and re-layouts  36.9 us (2%)
  matrix products  30.3 us (2%)
    all_gather x2, waiting for transfers between devices, spread(): return jnp.sum(lax.all_gather(kept, axis), axis=0)  1420 us
    sub x1, other arithmetic, chebyshev(): 2.0 * (hamiltonian(current, widen(current), potential) - 6.0 * current)  60.1 us
    select_n x2, other arithmetic, spread(): jnp.where(lax.axis_index(axis) == source, value, 0).astype(value.dtype)  58.4 us
    div x1, other arithmetic, chebyshev(): current = (hamiltonian(block, widen(block), potential) - 6.0 * block) / 5.0  55.2 us
    ppermute x3, waiting for transfers between devices, extended_2(): before = lax.ppermute(last, axis, up)  55.1 us
    ppermute x3, waiting for transfers between devices, extended_2(): after = lax.ppermute(first, axis, down)  37.9 us
  transfers between devices with their start and end apart: 8, of which 8 were waited for; matrix products, arithmetic and copies ran while one was open for 2% of the time, Pallas kernels for 0%

profile of v1, /device:TPU:4, one launch (start us, length us, event | category | flops | bytes accessed | tf_op | source)
XLA Modules:
  0.0 1855.1 jit_solution(7198638686056092427)
XLA Ops:
  7.2 0.0 copy-start
  7.2 0.0 all-gather.7.cloned.1.call-start
  7.2 4.1 copy.24
  11.4 0.0 copy-start.5
  11.4 0.9 fusion.175
  12.3 1.3 copy-done.1
  13.6 7.9 collective-permute-start
  21.5 0.8 fusion.157
  22.3 0.8 fusion.155
  23.1 0.8 fusion.153
  23.9 0.8 fusion.151
  24.7 23.2 %collective-permute-done = f32[4,4,36864]{2,1,0:T(4,128)S(1)} collective-permute-done((f32[4,4,36864]{2,1,0:T(4,128)S(1)}, f32[4,4,36864]{2,1,0:T(4,128)S(1)}, u32[]{:S(2)}, u32[]{:S(2)}) %collective-permute-start) | collective-permute-done | bytes 2359328 | tf_op jit(solution)/shard_map/ppermute | solution.py:19
  47.9 5.7 collective-permute-done.1
  53.6 55.2 %broadcast_multiply_fusion = (f32[4,6,36864]{2,1,0:T(8,128)}, f32[4,6,36864]{2,1,0:T(8,128)}) fusion(f32[4,6,36864]{2,1,0:T(8,128)} %copy-done.1, f32[6,36864]{1,0:T(8,128)S(1)} %copy-done.5, f32[36864]{0:T(1024)} %get-tuple-element.32, f32[36864]{0:T(1024)} %get-tuple-element.31, f32[4,4,36864]{2,1,0:T(4,128)} %collective-permute-done.1, ...), kind=kLoop, calls=%fused_computation.233 | loop fusion | flops 52199424 | bytes 17399808 | tf_op jit(solution)/shard_map/div | solution.py:57
  108.7 0.0 copy-start.6
  108.7 0.0 copy-start.2
  108.8 5.0 fusion.174
  113.7 0.3 collective-permute-start.2
  114.0 15.2 collective-permute-start.3
  129.2 1.1 broadcast_multiply_fusion.1
  130.3 10.1 collective-permute-done.2
  140.4 24.1 %collective-permute-done.3 = f32[4,4,36864]{2,1,0:T(4,128)} collective-permute-done((f32[4,4,36864]{2,1,0:T(4,128)S(1)}, f32[4,4,36864]{2,1,0:T(4,128)}, u32[]{:S(2)}, u32[]{:S(2)}) %collective-permute-start.3) | collective-permute-done | bytes 2359328 | tf_op jit(solution)/shard_map/ppermute | solution.py:18
  164.5 60.1 %fusion.42 = f32[4,6,36864]{2,1,0:T(8,128)} fusion(f32[4,6,36864]{2,1,0:T(8,128)} %get-tuple-element.9, f32[4,4,36864]{2,1,0:T(4,128)} %collective-permute-done.3, f32[4,4,36864]{2,1,0:T(4,128)} %collective-permute-done.2, f32[4,6,36864]{2,1,0:T(8,128)} %get-tuple-element.10, f32[6,36864]{1,0:T(8,128)} %broadcast_multiply_fusion.1, ...), kind=kLoop, calls=%fused_computation.84 | loop fusion | flops 53084160 | bytes 20938752 | tf_op jit(solution)/shard_map/sub | solution.py:60
  224.5 0.0 copy-start.7
  224.5 7.1 fusion.173
  231.6 20.1 %collective-permute-start.5 = (f32[4,4,36864]{2,1,0:T(4,128)}, f32[4,4,36864]{2,1,0:T(4,128)}, u32[]{:S(2)}, u32[]{:S(2)}) collective-permute-start(f32[4,4,36864]{2,1,0:T(4,128)} %get-tuple-element.12), channel_id=1, source_target_pairs={{0,8},{8,16},{16,24},{24,32},{32,40},{40,48},{48,56},{56,64},{64,7... | collective-permute-start | bytes 7077896 | tf_op jit(solution)/shard_map/ppermute | solution.py:18
  251.7 0.7 and_select_fusion
  252.4 0.6 fusion.176
  253.6 4.7 collective-permute-done.4
  258.3 25.4 %collective-permute-done.5 = f32[4,4,36864]{2,1,0:T(4,128)} collective-permute-done((f32[4,4,36864]{2,1,0:T(4,128)}, f32[4,4,36864]{2,1,0:T(4,128)}, u32[]{:S(2)}, u32[]{:S(2)}) %collective-permute-start.5) | collective-permute-done | bytes 2359328 | tf_op jit(solution)/shard_map/ppermute | solution.py:18
  283.7 55.7 %broadcast_select_fusion = (f32[4,6,36864]{2,1,0:T(8,128)}, f32[4,6,36864]{2,1,0:T(8,128)}) fusion(pred[]{:T(512)S(6)} %eq.15, f32[4,6,36864]{2,1,0:T(8,128)} %get-tuple-element.10, f32[4,6,36864]{2,1,0:T(8,128)} %fusion.42, f32[6,36864]{1,0:T(8,128)S(1)} %copy-done.7, f32[36864]{0:T(1024)} %get-tuple-element.32, f32[36864]{0:T(1024)} %get-tuple-element.31, ...), kind=kLoop, calls=%fused_computation.231 | loop fusion | flops 54853632 | bytes 20938752 | tf_op jit(solution)/shard_map/jit(_where)/select_n | solution.py:25
  339.4 0.0 all-gather.7.cloned.1.call-update
  339.5 0.0 all-gather.5.cloned.1.call-start
  340.1 2.6 broadcast_select_fusion.1
  342.8 0.0 all-gather.5.cloned.1.call-update
  345.4 4.6 copy.42
  350.0 0.0 copy-start.4
  350.0 1.8 copy-done.4
  351.8 8.1 fusion.162
  359.9 721.0 %all-gather.7.cloned.1.call-done = f32[32,6,36864]{2,1,0:T(8,128)} async-done(((f32[4,6,36864]{2,1,0:T(8,128)}), f32[32,6,36864]{2,1,0:T(8,128)}) %all-gather.7.cloned.1.call-update) | async-done | bytes 28311568 | tf_op jit(solution)/shard_map/all_gather | solution.py:26
  1080.9 16.3 reduce_sum.19
  1097.2 6.9 copy.40
  1104.1 701.0 %all-gather.5.cloned.1.call-done = f32[32,6,36864]{2,1,0:T(8,128)} async-done(((f32[4,6,36864]{2,1,0:T(8,128)}), f32[32,6,36864]{2,1,0:T(8,128)}) %all-gather.5.cloned.1.call-update) | async-done | bytes 28311568 | tf_op jit(solution)/shard_map/all_gather | solution.py:26
  1805.1 16.2 reduce_sum.18
  1821.3 4.6 copy.37
  1825.9 0.0 copy-start.3
  1825.9 10.4 convolution_add_fusion.1
  1836.4 11.7 convolution_add_fusion
  (9 shorter events, 0.0 us)
Async XLA Ops:
  7.2 344.6 %copy-start = (f32[32,32]{1,0:T(8,128)S(1)}, f32[32,32]{1,0:T(8,128)}, u32[]{:S(2)}) copy-start(f32[32,32]{1,0:T(8,128)} %param.8) | copy-start | bytes 12292
  7.2 1073.7 %all-gather.7.cloned.1.call-start = ((), (), s32[]{:S(2)}) async-start(), calls=%async_computation.1 | async-start | bytes 42467328 | tf_op jit(solution)/shard_map/all_gather | solution.py:26
  11.4 2.2 copy-start.1
  11.4 42.2 %copy-start.5 = (f32[6,36864]{1,0:T(8,128)S(1)}, f32[6,36864]{1,0:T(8,128)}, u32[]{:S(2)}) copy-start(f32[6,36864]{1,0:T(8,128)} %param.7) | copy-start | bytes 2654212
  13.6 34.3 %collective-permute-start = (f32[4,4,36864]{2,1,0:T(4,128)S(1)}, f32[4,4,36864]{2,1,0:T(4,128)S(1)}, u32[]{:S(2)}, u32[]{:S(2)}) collective-permute-start(f32[4,4,36864]{2,1,0:T(4,128)S(1)} %get-tuple-element.15), channel_id=1, source_target_pairs={{8,0},{16,8},{24,16},{32,24},{40,32},{48,40},{56,48},{64,56},{72,6... | collective-permute-start | bytes 7077896 | tf_op jit(solution)/shard_map/ppermute | solution.py:19
  21.5 32.1 %collective-permute-start.1 = (f32[4,4,36864]{2,1,0:T(4,128)S(1)}, f32[4,4,36864]{2,1,0:T(4,128)}, u32[]{:S(2)}, u32[]{:S(2)}) collective-permute-start(f32[4,4,36864]{2,1,0:T(4,128)S(1)} %get-tuple-element.16), channel_id=1, source_target_pairs={{0,8},{8,16},{16,24},{24,32},{32,40},{40,48},{48,56},{56,64},{64,7... | collective-permute-start | bytes 7077896 | tf_op jit(solution)/shard_map/ppermute | solution.py:18
  108.7 20.4 %copy-start.6 = (f32[6,36864]{1,0:T(8,128)S(1)}, f32[6,36864]{1,0:T(8,128)}, u32[]{:S(2)}) copy-start(f32[6,36864]{1,0:T(8,128)} %param.7) | copy-start | bytes 2654212
  108.7 55.7 %copy-start.2 = (f32[4,6,36864]{2,0,1:T(4,128)S(1)}, f32[4,6,36864]{2,0,1:T(4,128)}, u32[]{:S(2)}) copy-start(f32[4,6,36864]{2,0,1:T(4,128)} %param.6) | copy-start | bytes 10616836
  113.7 26.7 %collective-permute-start.2 = (f32[4,4,36864]{2,1,0:T(4,128)S(1)}, f32[4,4,36864]{2,1,0:T(4,128)}, u32[]{:S(2)}, u32[]{:S(2)}) collective-permute-start(f32[4,4,36864]{2,1,0:T(4,128)S(1)} %get-tuple-element.13), channel_id=1, source_target_pairs={{8,0},{16,8},{24,16},{32,24},{40,32},{48,40},{56,48},{64,56},{72,6... | collective-permute-start | bytes 7077896 | tf_op jit(solution)/shard_map/ppermute | solution.py:19
  114.0 50.5 %collective-permute-start.3 = (f32[4,4,36864]{2,1,0:T(4,128)S(1)}, f32[4,4,36864]{2,1,0:T(4,128)}, u32[]{:S(2)}, u32[]{:S(2)}) collective-permute-start(f32[4,4,36864]{2,1,0:T(4,128)S(1)} %get-tuple-element.14), channel_id=1, source_target_pairs={{0,8},{8,16},{16,24},{24,32},{32,40},{40,48},{48,56},{56,64},{64,7... | collective-permute-start | bytes 7077896 | tf_op jit(solution)/shard_map/ppermute | solution.py:18
  224.5 59.2 %copy-start.7 = (f32[6,36864]{1,0:T(8,128)S(1)}, f32[6,36864]{1,0:T(8,128)}, u32[]{:S(2)}) copy-start(f32[6,36864]{1,0:T(8,128)} %param.7) | copy-start | bytes 2654212
  231.6 26.7 %collective-permute-start.4 = (f32[4,4,36864]{2,1,0:T(4,128)}, f32[4,4,36864]{2,1,0:T(4,128)S(1)}, u32[]{:S(2)}, u32[]{:S(2)}) collective-permute-start(f32[4,4,36864]{2,1,0:T(4,128)} %get-tuple-element.11), channel_id=1, source_target_pairs={{8,0},{16,8},{24,16},{32,24},{40,32},{48,40},{56,48},{64,56},{72,6... | collective-permute-start | bytes 7077896 | tf_op jit(solution)/shard_map/ppermute | solution.py:19
  231.6 52.0 %collective-permute-start.5 = (f32[4,4,36864]{2,1,0:T(4,128)}, f32[4,4,36864]{2,1,0:T(4,128)}, u32[]{:S(2)}, u32[]{:S(2)}) collective-permute-start(f32[4,4,36864]{2,1,0:T(4,128)} %get-tuple-element.12), channel_id=1, source_target_pairs={{0,8},{8,16},{16,24},{24,32},{32,40},{40,48},{48,56},{56,64},{64,7... | collective-permute-start | bytes 7077896 | tf_op jit(solution)/shard_map/ppermute | solution.py:18
  339.5 1465.6 %all-gather.5.cloned.1.call-start = ((), (), s32[]{:S(2)}) async-start(), calls=%async_computation | async-start | bytes 42467328 | tf_op jit(solution)/shard_map/all_gather | solution.py:26
  350.0 1.8 copy-start.4
  1825.9 10.5 copy-start.3
Sparse Core Ops, SparseCore 0:
  339.6 741.2 all-gather.6
  1082.7 722.3 all-gather.4
